TPU v7x, 128 devices: a whole 4x4x4 slice. The times are simulated.
128 devices in a mesh: ctx: 16 (over y_hi, x, core), tp: 8 (over y_lo, z).
Axes of the slice: x: 4, y: 4 (y_hi: 2, y_lo: 2; y = y_hi * 2 + y_lo), z: 4, core: 2. Of those that a mesh axis runs over, the one named last changes fastest.
Arguments:
- tokens: bfloat16 [2048, 4096], P('ctx', 'tp'), may hold values from -6 to 6
- in_weight: bfloat16 [4096, 3, 4096], P(None, None, 'tp'), may hold values from -0.09375 to 0.09375
- conv_weight: float32 [7, 3, 4096], P(None, None, 'tp'), may hold values from -2 to 2
- filters: bfloat16 [2048, 4096], P(None, 'tp'), may hold values from -1 to 1
- skip_gain: float32 [4096], P('tp'), may hold values from -4 to 4
Outputs:
- mixed_out: bfloat16 [2048, 4096], P('ctx', 'tp')
All inputs are finite; a program needn't handle non-finite values.
Results may differ from a plain program's by a relative error of at most 0.0095.
Values may be sent and summed in bfloat16 or wider, within the bound.
A program may use at most 128 MiB of HBM per device.

v0:
```python
import math
import jax
import jax.numpy as jnp
from jax import lax
from jax.sharding import PartitionSpec as P

TAPS = 7


def passed_along(value, axis, steps):
    count = lax.axis_size(axis)
    leading, last = (max(0, -steps), min(count, count - steps))
    return lax.ppermute(value, axis, [(source, source + steps) for source in range(leading, last)])


def exact_dot(left, right):
    return jnp.dot(left, right, precision=lax.Precision.HIGHEST, preferred_element_type=jnp.float32)


def split_table(table):
    high = table.astype(jnp.bfloat16)
    low = (table - high.astype(jnp.float32)).astype(jnp.bfloat16)
    return (high, low)


def local(tokens, in_weight, conv_weight, filters, skip_gain):
    block_rows = tokens.shape[0]
    channels = in_weight.shape[2]
    flat_weight = in_weight.reshape(in_weight.shape[0], 3 * channels)
    gathered = lax.all_gather(tokens, "tp", axis=1, tiled=True)
    summed = jnp.dot(gathered, flat_weight, preferred_element_type=jnp.float32)
    projected = summed.astype(jnp.bfloat16).reshape(block_rows, 3, channels)
    earlier = passed_along(projected[block_rows - (TAPS - 1) :], "ctx", 1)
    extended = jnp.concatenate([earlier, projected], 0).astype(jnp.float32)
    branches = conv_weight[0] * extended[0:block_rows]
    for tap_index in range(1, TAPS):
        branches = branches + conv_weight[tap_index] * extended[tap_index : tap_index + block_rows]
    gate_branch = branches[:, 0]
    product = (branches[:, 1] * branches[:, 2]).astype(jnp.bfloat16)
    product_wide = product.astype(jnp.float32)
    sub_rows = block_rows // 2
    dft_length = 2 * sub_rows
    frequency = jnp.arange(sub_rows, dtype=jnp.int32)
    position = jnp.arange(sub_rows, dtype=jnp.int32)
    step_angle = 2.0 * math.pi / dft_length
    angles = (frequency[:, None] * position[None, :] % dft_length).astype(jnp.float32) * step_angle
    cos_high, cos_low = split_table(jnp.cos(angles))
    sin_high, sin_low = split_table(-jnp.sin(angles))
    alternate = jnp.where(frequency % 2 == 0, 1.0, -1.0).astype(jnp.float32)[:, None]
    nyquist_sign = jnp.where(position % 2 == 0, 1.0, -1.0).astype(jnp.bfloat16)
    nyquist_alternate = 1.0
    back_angles = ((position[:, None] + sub_rows) * frequency[None, :] % dft_length).astype(
        jnp.float32
    ) * step_angle
    back_weights = jnp.where(frequency == 0, 1.0, 2.0).astype(jnp.float32)[None, :]
    cos_back = jnp.cos(back_angles) * back_weights
    sin_back = jnp.sin(back_angles) * back_weights
    nyquist_back = jnp.where((position + sub_rows) % 2 == 0, 1.0, -1.0).astype(jnp.float32)

    def spectrum(data):
        real_part = jnp.einsum(
            "ks,hsc->hkc", cos_high, data, preferred_element_type=jnp.float32
        ) + jnp.einsum("ks,hsc->hkc", cos_low, data, preferred_element_type=jnp.float32)
        imag_part = jnp.einsum(
            "ks,hsc->hkc", sin_high, data, preferred_element_type=jnp.float32
        ) + jnp.einsum("ks,hsc->hkc", sin_low, data, preferred_element_type=jnp.float32)
        nyquist = jnp.einsum("s,hsc->hc", nyquist_sign, data, preferred_element_type=jnp.float32)
        return (real_part, imag_part, nyquist)

    blocks = filters.shape[0] // sub_rows
    filter_real, filter_imag, filter_nyquist = spectrum(filters.reshape(blocks, sub_rows, channels))
    padded_real = jnp.concatenate([jnp.zeros((1, sub_rows, channels), jnp.float32), filter_real], 0)
    padded_imag = jnp.concatenate([jnp.zeros((1, sub_rows, channels), jnp.float32), filter_imag], 0)
    padded_nyquist = jnp.concatenate([jnp.zeros((1, channels), jnp.float32), filter_nyquist], 0)
    own_index = lax.axis_index("ctx")

    def gain_at(distance):
        causal = (distance >= 0).astype(jnp.float32)
        lag_index = jnp.clip(distance, 0, blocks - 1)
        gain_real = lax.dynamic_index_in_dim(
            padded_real, lag_index, 0, keepdims=False
        ) + alternate * lax.dynamic_index_in_dim(padded_real, lag_index + 1, 0, keepdims=False)
        gain_imag = lax.dynamic_index_in_dim(
            padded_imag, lag_index, 0, keepdims=False
        ) + alternate * lax.dynamic_index_in_dim(padded_imag, lag_index + 1, 0, keepdims=False)
        gain_nyquist = lax.dynamic_index_in_dim(
            padded_nyquist, lag_index, 0, keepdims=False
        ) + nyquist_alternate * lax.dynamic_index_in_dim(
            padded_nyquist, lag_index + 1, 0, keepdims=False
        )
        return (causal * gain_real, causal * gain_imag, causal * gain_nyquist)

    def add_term(running, source_real, source_imag, source_nyquist, source_block):
        next_real, next_imag, next_nyquist = ([], [], [])
        for target in range(2):
            total_real = running[0][target]
            total_imag = running[1][target]
            total_nyquist = running[2][target]
            for half in range(2):
                gain_real, gain_imag, gain_nyquist = gain_at(
                    2 * (own_index - source_block) + target - half
                )
                total_real = (
                    total_real + gain_real * source_real[half] - gain_imag * source_imag[half]
                )
                total_imag = (
                    total_imag + gain_real * source_imag[half] + gain_imag * source_real[half]
                )
                total_nyquist = total_nyquist + gain_nyquist * source_nyquist[half]
            next_real.append(total_real)
            next_imag.append(total_imag)
            next_nyquist.append(total_nyquist)
        return (jnp.stack(next_real), jnp.stack(next_imag), jnp.stack(next_nyquist))

    initial = (
        jnp.zeros((2, sub_rows, channels), jnp.float32),
        jnp.zeros((2, sub_rows, channels), jnp.float32),
        jnp.zeros((2, channels), jnp.float32),
    )
    shard_part = lax.all_gather(product[None], "ctx", axis=0, tiled=True)

    def visit_member(member, state):
        block_data = lax.dynamic_index_in_dim(shard_part, member, 0, keepdims=False).reshape(
            2, sub_rows, channels
        )
        source_real, source_imag, source_nyquist = spectrum(block_data)
        return add_term(state, source_real, source_imag, source_nyquist, member)

    totals = lax.fori_loop(0, shard_part.shape[0], visit_member, initial)
    halves = []
    for target in range(2):
        halves.append(
            exact_dot(cos_back, totals[0][target])
            - exact_dot(sin_back, totals[1][target])
            + nyquist_back[:, None] * totals[2][target][None, :]
        )
    convolved = jnp.concatenate(halves, 0) / dft_length
    return (gate_branch * (convolved + skip_gain * product_wide)).astype(jnp.bfloat16)


def solution(mesh):
    placed = (P("ctx", "tp"), P(None, None, "tp"), P(None, None, "tp"), P(None, "tp"), P("tp"))
    return jax.shard_map(
        local, mesh=mesh, in_specs=placed, out_specs=P("ctx", "tp"), check_vma=False
    )
```

profile of v0, /device:TPU:1, one launch (start us, length us, event | category | flops | bytes accessed | tf_op | source)
XLA Modules:
  0.0 261.4 jit_solution(9611068512065455228)
XLA Ops:
  7.3 17.0 %copy.8 = bf16[4096,3,512]{0,2,1:T(8,128)(2,1)} copy(bf16[4096,3,512]{2,0,1:T(8,128)(2,1)} %param.8) | data formatting | bytes 25165824 | tf_op args[1]
  24.3 22.3 %all-gather.4.cloned.1.call-done = bf16[128,4096]{1,0:T(8,128)(2,1)} async-done(((bf16[128,512]{1,0:T(8,128)(2,1)}), bf16[128,4096]{1,0:T(8,128)(2,1)}) %all-gather.4.cloned.1.call-update) | async-done | bytes 1048592 | tf_op jit(solution)/shard_map/all_gather | solution.py:30
  46.7 9.2 %convolution_convert_fusion = bf16[128,1536]{1,0:T(8,128)(2,1)S(1)} fusion(bf16[128,4096]{1,0:T(8,128)(2,1)} %all-gather.4.cloned.1.call-done, bf16[4096,1536]{0,1:T(8,128)(2,1)} %bitcast.142), kind=kOutput, calls=%fused_computation.99 | convolution fusion | flops 1610809344 | bytes 14024704 | tf_op jit(solution)/shard_map/dot_general | solution.py:31
  55.9 8.4 %collective-permute-start = (bf16[6,3,512]{2,0,1:T(8,128)(2,1)S(1)}, bf16[6,3,512]{2,0,1:T(8,128)(2,1)S(1)}, u32[]{:S(2)}, u32[]{:S(2)}) collective-permute-start(bf16[6,3,512]{2,0,1:T(8,128)(2,1)S(1)} %bitcast.148), channel_id=1, source_target_pairs={{0,8},{8,16},{16,24},{24,32},{32,40},{40,48},{48,56},{56,64},{64,7... | collective-permute-start | bytes 55304 | tf_op jit(solution)/shard_map/ppermute | solution.py:13
  69.6 2.6 concatenate.16
  73.8 2.6 %concatenate.17 = f32[33,64,512]{2,1,0:T(8,128)} pad(f32[32,64,512]{2,1,0:T(8,128)S(1)} %add_bitcast_fusion, f32[]{:T(128)} %constant.212.clone.1), padding=1_0x0_0x0_0 | pad | bytes 8519684 | tf_op jit(solution)/shard_map/concatenate | solution.py:73
  77.7 39.6 %all-gather.6.cloned.1.call-done = bf16[2048,1,512]{2,0,1:T(8,128)(2,1)} async-done(((bf16[128,1,512]{2,0,1:T(8,128)(2,1)}), bf16[2048,1,512]{2,0,1:T(8,128)(2,1)}) %all-gather.6.cloned.1.call-update) | async-done | bytes 2097168 | tf_op jit(solution)/shard_map/all_gather | solution.py:120
  118.1 130.9 %while.24 = (s32[]{:T(128)}, f32[2,64,512]{2,1,0:T(8,128)S(1)}, f32[2,64,512]{2,1,0:T(8,128)}, f32[2,512]{1,0:T(2,128)S(1)}, s32[]{:T(128)}, /*index=5*/f32[33,6...) while((s32[]{:T(128)}, f32[2,64,512]{2,1,0:T(8,128)S(1)}, ...), condition=%wide.region_1.2_spmd.clone.clone, body=%wide.region_0.1_spmd.clone.clone.sunk | while | flops 36070464 | bytes 9090577 | solution.py:129
  120.2 1.6 multiply_add_fusion.5
  121.8 1.2 multiply_subtract_fusion.3
  123.0 1.4 multiply_add_fusion.6
  128.4 1.6 multiply_add_fusion.5
  129.9 1.2 multiply_subtract_fusion.3
  131.2 1.4 multiply_add_fusion.6
  133.4 1.0 add_add_fusion.2
  136.6 1.6 multiply_add_fusion.5
  138.1 1.2 multiply_subtract_fusion.3
  139.4 1.4 multiply_add_fusion.6
  141.6 1.0 add_add_fusion.2
  144.7 1.6 multiply_add_fusion.5
  146.3 1.2 multiply_subtract_fusion.3
  147.6 1.4 multiply_add_fusion.6
  149.8 1.0 add_add_fusion.2
  152.9 1.6 multiply_add_fusion.5
  154.5 1.2 multiply_subtract_fusion.3
  155.7 1.4 multiply_add_fusion.6
  161.1 1.6 multiply_add_fusion.5
  162.7 1.2 multiply_subtract_fusion.3
  163.9 1.4 multiply_add_fusion.6
  169.3 1.6 multiply_add_fusion.5
  170.9 1.2 multiply_subtract_fusion.3
  172.1 1.4 multiply_add_fusion.6
  177.5 1.6 multiply_add_fusion.5
  179.1 1.2 multiply_subtract_fusion.3
  180.3 1.4 multiply_add_fusion.6
  182.5 1.0 add_add_fusion.2
  185.7 1.6 multiply_add_fusion.5
  187.2 1.2 multiply_subtract_fusion.3
  188.5 1.4 multiply_add_fusion.6
  190.7 1.0 add_add_fusion.2
  193.9 1.6 multiply_add_fusion.5
  195.4 1.2 multiply_subtract_fusion.3
  196.7 1.4 multiply_add_fusion.6
  202.0 1.6 multiply_add_fusion.5
  203.6 1.2 multiply_subtract_fusion.3
  204.9 1.4 multiply_add_fusion.6
  210.2 1.6 multiply_add_fusion.5
  211.8 1.2 multiply_subtract_fusion.3
  213.0 1.4 multiply_add_fusion.6
  218.4 1.6 multiply_add_fusion.5
  220.0 1.2 multiply_subtract_fusion.3
  221.2 1.4 multiply_add_fusion.6
  226.6 1.6 multiply_add_fusion.5
  228.2 1.2 multiply_subtract_fusion.3
  229.4 1.4 multiply_add_fusion.6
  234.8 1.6 multiply_add_fusion.5
  236.4 1.2 multiply_subtract_fusion.3
  237.6 1.4 multiply_add_fusion.6
  243.0 1.6 multiply_add_fusion.5
  244.5 1.2 multiply_subtract_fusion.3
  245.8 1.4 multiply_add_fusion.6
  249.9 1.3 fusion.77
  251.3 1.4 fusion.78
  252.6 1.9 fusion.87
  (208 shorter events, 68.4 us)
Async XLA Ops:
  6.5 61.1 %copy-start = (bf16[2048,512]{1,0:T(8,128)(2,1)S(1)}, bf16[2048,512]{1,0:T(8,128)(2,1)}, u32[]{:S(2)}) copy-start(bf16[2048,512]{1,0:T(8,128)(2,1)} %param.10) | copy-start | bytes 6291460
  6.5 40.1 %all-gather.4.cloned.1.call-start = ((), (), s32[]{:S(2)}) async-start(), calls=%async_computation | async-start | bytes 1179648 | tf_op jit(solution)/shard_map/all_gather | solution.py:30
  7.3 17.0 %copy-start.2 = (f32[7,3,512]{2,0,1:T(8,128)S(1)}, f32[7,3,512]{2,0,1:T(8,128)}, u32[]{:S(2)}) copy-start(f32[7,3,512]{2,0,1:T(8,128)} %param.9) | copy-start | bytes 129028
  7.3 110.1 %all-gather.6.cloned.1.call-start = ((), (), s32[]{:S(2)}) async-start(), calls=%async_computation.1 | async-start | bytes 2228224 | tf_op jit(solution)/shard_map/all_gather | solution.py:120
  55.9 9.4 %collective-permute-start = (bf16[6,3,512]{2,0,1:T(8,128)(2,1)S(1)}, bf16[6,3,512]{2,0,1:T(8,128)(2,1)S(1)}, u32[]{:S(2)}, u32[]{:S(2)}) collective-permute-start(bf16[6,3,512]{2,0,1:T(8,128)(2,1)S(1)} %bitcast.148), channel_id=1, source_target_pairs={{0,8},{8,16},{16,24},{24,32},{32,40},{40,48},{48,56},{56,64},{64,7... | collective-permute-start | bytes 55304 | tf_op jit(solution)/shard_map/ppermute | solution.py:13
  66.0 0.9 copy-start.1
Sparse Core Ops, SparseCore 0:
  9.0 37.5 all-gather.3
  67.7 49.5 all-gather.5
where the time goes:
time: 264 us; the launch traced here: 261 us
  other arithmetic  97.9 us (37%)
  waiting for transfers between devices  63.2 us (24%)
  local copies, waits for them, and re-layouts  39.7 us (15%)
  matrix products  36.7 us (14%)
  between operations  13.6 us (5%)
  starting transfers between devices  8.48 us (3%)
    add x32, other arithmetic, add_term(): total_imag + gain_real * source_imag[half] + gain_imag * source_real[half]  46.9 us
    all_gather x1, waiting for transfers between devices, local(): shard_part = lax.all_gather(product[None], 'ctx', axis=0, tiled=True)  39.6 us
    all_gather x1, waiting for transfers between devices, local(): gathered = lax.all_gather(tokens, 'tp', axis=1, tiled=True)  22.3 us
    sub x16, other arithmetic, add_term(): total_real + gain_real * source_real[half] - gain_imag * source_imag[half]  19.5 us
    unnamed x11, local copies, waits for them, and re-layouts  17.9 us
    add x16, other arithmetic, add_term(): total_nyquist = total_nyquist + gain_nyquist * source_nyquist[half]  15.4 us
    dynamic_slice x16, local copies, waits for them, and re-layouts, visit_member(): lax.dynamic_index_in_dim(shard_part, member, 0, keepdims=False)  14.7 us
    another operation x32, other arithmetic, add_term(): return (jnp.stack(next_real), jnp.stack(next_imag), jnp.stack(next_nyquist))  12 us
  transfers between devices with their start and end apart: 3, of which 3 were waited for; matrix products, arithmetic and copies ran while one was open for 11% of the time, Pallas kernels for 0%

commit v1 on v0

--- a/solution.py
+++ b/solution.py
@@ -27,7 +27,10 @@
     block_rows = tokens.shape[0]
     channels = in_weight.shape[2]
     flat_weight = in_weight.reshape(in_weight.shape[0], 3 * channels)
-    gathered = lax.all_gather(tokens, "tp", axis=1, tiled=True)
+    size = lax.axis_size("tp")
+    pieces = jnp.stack([tokens for _ in range(size)])
+    pieces = lax.all_to_all(pieces, "tp", split_axis=0, concat_axis=0)
+    gathered = jnp.concatenate(pieces, axis=1)
     summed = jnp.dot(gathered, flat_weight, preferred_element_type=jnp.float32)
     projected = summed.astype(jnp.bfloat16).reshape(block_rows, 3, channels)
     earlier = passed_along(projected[block_rows - (TAPS - 1) :], "ctx", 1)

time: 264 us -> 249 us (0.943)
  waiting for transfers between devices: 63.2 us -> 41.4 us
  local copies, waits for them, and re-layouts: 39.7 us -> 43.8 us
    all_gather x1 -> x0, waiting for transfers between devices: 22.3 us -> none  [local(): gathered = lax.all_gather(tokens, 'tp', axis=1, tiled=True)]
    all_to_all x0 -> x1, starting transfers between devices: none -> 6.88 us  [local(): pieces = lax.all_to_all(pieces, 'tp', split_axis=0, concat_axis=0)]
    ppermute x1, starting transfers between devices: 8.43 us -> 4.13 us  [passed_along(): lax.ppermute(value, axis, [(source, source + steps) for source in range(l...]
    unnamed x11 -> x14, local copies, waits for them, and re-layouts: 17.9 us -> 19.8 us
  transfers between devices with their start and end apart: 3 -> 3, of which waited for: 3 -> 1; matrix products, arithmetic and copies ran while one was open for 11% -> 12% of each run, Pallas kernels for 0% -> 0%
where the time goes in v1:
time: 249 us; the launch traced here: 246 us
  other arithmetic  98 us (39%)
  local copies, waits for them, and re-layouts  43.8 us (18%)
  waiting for transfers between devices  41.4 us (17%)
  matrix products  36.3 us (15%)
  between operations  13.6 us (5%)
  starting transfers between devices  11.1 us (4%)
    add x32, other arithmetic, add_term(): total_imag + gain_real * source_imag[half] + gain_imag * source_real[half]  46.9 us
    all_gather x1, waiting for transfers between devices, local(): shard_part = lax.all_gather(product[None], 'ctx', axis=0, tiled=True)  41.4 us
    unnamed x14, local copies, waits for them, and re-layouts  19.8 us
    sub x16, other arithmetic, add_term(): total_real + gain_real * source_real[half] - gain_imag * source_imag[half]  19.5 us
    add x16, other arithmetic, add_term(): total_nyquist = total_nyquist + gain_nyquist * source_nyquist[half]  15.4 us
    dynamic_slice x16, local copies, waits for them, and re-layouts, visit_member(): lax.dynamic_index_in_dim(shard_part, member, 0, keepdims=False)  14.7 us
    another operation x32, other arithmetic, add_term(): return (jnp.stack(next_real), jnp.stack(next_imag), jnp.stack(next_nyquist))  12.1 us
    dot_general x1, matrix products, local(): summed = jnp.dot(gathered, flat_weight, preferred_element_type=jnp.float32)  8.88 us
  transfers between devices with their start and end apart: 3, of which 1 were waited for; matrix products, arithmetic and copies ran while one was open for 12% of the time, Pallas kernels for 0%

profile of v1, /device:TPU:1, one launch (start us, length us, event | category | flops | bytes accessed | tf_op | source)
XLA Modules:
  0.0 245.9 jit_solution(12972545775239337957)
XLA Ops:
  6.5 1.2 copy.8
  7.7 1.2 stack.71
  8.9 6.9 %all-to-all-start = ((bf16[8,128,512]{1,2,0:T(8,128)(2,1)}), bf16[8,128,512]{1,2,0:T(8,128)(2,1)S(1)}, u32[]{:S(2)}, u32[]{:S(2)}) async-start(bf16[8,128,512]{1,2,0:T(8,128)(2,1)} %stack.71), calls=%async_computation | async-start | bytes 2097152 | tf_op jit(solution)/shard_map/all_to_all | solution.py:32
  15.8 17.0 %copy.9 = bf16[4096,3,512]{0,2,1:T(8,128)(2,1)} copy(bf16[4096,3,512]{2,0,1:T(8,128)(2,1)} %param.8) | data formatting | bytes 25165824 | tf_op args[1]
  32.8 8.9 %convolution_convert_fusion = bf16[128,1536]{1,0:T(8,128)(2,1)S(1)} fusion(bf16[128,4096]{0,1:T(8,128)(2,1)S(1)} %bitcast.146, bf16[4096,1536]{0,1:T(8,128)(2,1)} %bitcast.145), kind=kOutput, calls=%fused_computation.99 | convolution fusion | flops 1610809344 | bytes 14024704 | tf_op jit(solution)/shard_map/dot_general | solution.py:34
  42.5 4.1 %collective-permute-start = (bf16[6,3,512]{2,0,1:T(8,128)(2,1)S(1)}, bf16[6,3,512]{2,0,1:T(8,128)(2,1)S(1)}, u32[]{:S(2)}, u32[]{:S(2)}) collective-permute-start(bf16[6,3,512]{2,0,1:T(8,128)(2,1)S(1)} %bitcast.152), channel_id=1, source_target_pairs={{0,8},{8,16},{16,24},{24,32},{32,40},{40,48},{48,56},{56,64},{64,7... | collective-permute-start | bytes 55304 | tf_op jit(solution)/shard_map/ppermute | solution.py:13
  46.7 1.2 copy.11
  52.5 2.6 %concatenate.16 = f32[33,64,512]{2,1,0:T(8,128)} pad(f32[32,64,512]{2,1,0:T(8,128)S(1)} %add_bitcast_fusion.1, f32[]{:T(128)} %constant.212.clone.1), padding=1_0x0_0x0_0 | pad | bytes 8519684 | tf_op jit(solution)/shard_map/concatenate | solution.py:75
  56.7 2.6 %concatenate.17 = f32[33,64,512]{2,1,0:T(8,128)} pad(f32[32,64,512]{2,1,0:T(8,128)S(1)} %add_bitcast_fusion, f32[]{:T(128)} %constant.212.clone.1), padding=1_0x0_0x0_0 | pad | bytes 8519684 | tf_op jit(solution)/shard_map/concatenate | solution.py:76
  60.5 41.4 %all-gather.3.cloned.1.call-done = bf16[2048,1,512]{2,0,1:T(8,128)(2,1)} async-done(((bf16[128,1,512]{2,0,1:T(8,128)(2,1)}), bf16[2048,1,512]{2,0,1:T(8,128)(2,1)}) %all-gather.3.cloned.1.call-update) | async-done | bytes 2097168 | tf_op jit(solution)/shard_map/all_gather | solution.py:123
  102.7 130.9 %while.24 = (s32[]{:T(128)}, f32[2,64,512]{2,1,0:T(8,128)S(1)}, f32[2,64,512]{2,1,0:T(8,128)}, f32[2,512]{1,0:T(2,128)S(1)}, s32[]{:T(128)}, /*index=5*/f32[33,6...) while((s32[]{:T(128)}, f32[2,64,512]{2,1,0:T(8,128)S(1)}, ...), condition=%wide.region_1.2_spmd.clone.clone, body=%wide.region_0.1_spmd.clone.clone.sunk | while | flops 36070464 | bytes 9090577 | solution.py:132
  104.8 1.6 multiply_add_fusion.5
  106.3 1.2 multiply_subtract_fusion.3
  107.6 1.4 multiply_add_fusion.6
  112.9 1.6 multiply_add_fusion.5
  114.5 1.2 multiply_subtract_fusion.3
  115.7 1.4 multiply_add_fusion.6
  121.1 1.6 multiply_add_fusion.5
  122.7 1.2 multiply_subtract_fusion.3
  123.9 1.4 multiply_add_fusion.6
  129.3 1.6 multiply_add_fusion.5
  130.9 1.2 multiply_subtract_fusion.3
  132.1 1.4 multiply_add_fusion.6
  134.4 1.0 add_add_fusion.2
  137.5 1.6 multiply_add_fusion.5
  139.1 1.2 multiply_subtract_fusion.3
  140.3 1.4 multiply_add_fusion.6
  142.6 1.0 add_add_fusion.2
  145.7 1.6 multiply_add_fusion.5
  147.2 1.2 multiply_subtract_fusion.3
  148.5 1.4 multiply_add_fusion.6
  153.9 1.6 multiply_add_fusion.5
  155.4 1.2 multiply_subtract_fusion.3
  156.7 1.4 multiply_add_fusion.6
  162.0 1.6 multiply_add_fusion.5
  163.6 1.2 multiply_subtract_fusion.3
  164.9 1.4 multiply_add_fusion.6
  170.2 1.6 multiply_add_fusion.5
  171.8 1.2 multiply_subtract_fusion.3
  173.0 1.4 multiply_add_fusion.6
  178.4 1.6 multiply_add_fusion.5
  180.0 1.2 multiply_subtract_fusion.3
  181.2 1.4 multiply_add_fusion.6
  186.6 1.6 multiply_add_fusion.5
  188.2 1.2 multiply_subtract_fusion.3
  189.4 1.4 multiply_add_fusion.6
  194.8 1.6 multiply_add_fusion.5
  196.4 1.2 multiply_subtract_fusion.3
  197.6 1.4 multiply_add_fusion.6
  203.0 1.6 multiply_add_fusion.5
  204.5 1.2 multiply_subtract_fusion.3
  205.8 1.4 multiply_add_fusion.6
  211.2 1.6 multiply_add_fusion.5
  212.7 1.2 multiply_subtract_fusion.3
  214.0 1.4 multiply_add_fusion.6
  219.3 1.6 multiply_add_fusion.5
  220.9 1.2 multiply_subtract_fusion.3
  222.2 1.4 multiply_add_fusion.6
  227.5 1.6 multiply_add_fusion.5
  229.1 1.2 multiply_subtract_fusion.3
  230.3 1.4 multiply_add_fusion.6
  234.5 1.3 fusion.77
  235.9 1.4 fusion.78
  237.2 1.9 fusion.87
  (211 shorter events, 70.5 us)
Async XLA Ops:
  6.5 43.9 %copy-start = (bf16[2048,512]{1,0:T(8,128)(2,1)S(1)}, bf16[2048,512]{1,0:T(8,128)(2,1)}, u32[]{:S(2)}) copy-start(bf16[2048,512]{1,0:T(8,128)(2,1)} %param.10) | copy-start | bytes 6291460
  8.9 23.9 %all-to-all-start = ((bf16[8,128,512]{1,2,0:T(8,128)(2,1)}), bf16[8,128,512]{1,2,0:T(8,128)(2,1)S(1)}, u32[]{:S(2)}, u32[]{:S(2)}) async-start(bf16[8,128,512]{1,2,0:T(8,128)(2,1)} %stack.71), calls=%async_computation | async-start | bytes 2097152 | tf_op jit(solution)/shard_map/all_to_all | solution.py:32
  15.8 17.0 %copy-start.3 = (f32[7,3,512]{2,0,1:T(8,128)S(1)}, f32[7,3,512]{2,0,1:T(8,128)}, u32[]{:S(2)}) copy-start(f32[7,3,512]{2,0,1:T(8,128)} %param.9) | copy-start | bytes 129028
  15.8 86.1 %all-gather.3.cloned.1.call-start = ((), (), s32[]{:S(2)}) async-start(), calls=%async_computation.1 | async-start | bytes 2228224 | tf_op jit(solution)/shard_map/all_gather | solution.py:123
  41.7 0.8 copy-start.2
  42.5 5.6 %collective-permute-start = (bf16[6,3,512]{2,0,1:T(8,128)(2,1)S(1)}, bf16[6,3,512]{2,0,1:T(8,128)(2,1)S(1)}, u32[]{:S(2)}, u32[]{:S(2)}) collective-permute-start(bf16[6,3,512]{2,0,1:T(8,128)(2,1)S(1)} %bitcast.152), channel_id=1, source_target_pairs={{0,8},{8,16},{16,24},{24,32},{32,40},{40,48},{48,56},{56,64},{64,7... | collective-permute-start | bytes 55304 | tf_op jit(solution)/shard_map/ppermute | solution.py:13
  48.8 0.9 copy-start.1
Sparse Core Ops, SparseCore 0:
  50.6 51.2 all-gather.2
